TPU v7x, 32 devices: a whole 2x2x4 slice. The times are simulated.
32 devices in a mesh: grp: 2 (over y), tm: 4 (over z), row: 4 (over x, core).
Axes of the slice: x: 2, y: 2, z: 4, core: 2. Of those that a mesh axis runs over, the one named last changes fastest.
Arguments:
- frames: bfloat16 [16, 8, 24, 512], P(('grp', 'tm'), 'row'), parts along dimension 0, may hold values from -6 to 6
- w_in: bfloat16 [3, 3, 512, 512], P(None, None, None, ('tm', 'row')), may hold values from -0.046875 to 0.046875
- w_out: bfloat16 [3, 3, 512, 512], P(None, None, None, ('tm', 'row')), may hold values from -0.09375 to 0.09375
- decay_codes: int32 [512], replicated, may hold values from 0 to 15
- resets: int32 [16], P(('grp', 'tm')), parts along dimension 0, may hold values from 0 to 1, as said below
Outputs:
- mixed: bfloat16 [16, 8, 24, 512], P(('grp', 'tm'), 'row'), parts along dimension 0
There are 2 independent parts, one for each index of `grp`. A program takes and returns all parts, laid end to end along the dimension named above; an argument that names none is the same for every part. Nothing has to cross between parts.
Inputs may be any that keep to these rules, and one draw needn't show every extreme that they name: `decay_codes`: an entry of the table of 16 decays. `resets`: some frames start an episode and some do not.
All inputs are finite; a program needn't handle non-finite values.
Results may differ from a plain program's by a relative error of at most 0.005.
Values may be sent and summed in bfloat16 or wider, within the bound.
No kernel may reach another device: no remote copies, remote signals or barrier semaphores. Data moves between devices by JAX's collectives and lax.ppermute only.
A program may use at most 64 MiB of HBM per device.

v0:
```python
import math
import jax
import jax.numpy as jnp
from jax import lax
from jax.sharding import PartitionSpec as P

LEVELS = 16
WINDOW = 4096
LOW_LOG = math.log(0.995)
HIGH_LOG = math.log(0.9999)


def entering(part, axis, combine, identity):
    place = lax.axis_index(axis)
    gathered = jax.tree.map(lambda a: lax.all_gather(a, axis), part)
    state = jax.tree.map(lambda a, e: jnp.zeros_like(a) + jnp.asarray(e, a.dtype), part, identity)

    def one(turn, state):
        return combine(
            state, jax.tree.map(lambda a: lax.dynamic_index_in_dim(a, turn, 0, False), gathered)
        )

    return lax.fori_loop(0, place, one, state)


def extended_2(array, sides, width):
    for axis, dim in sides:
        size, length = (lax.axis_size(axis), array.shape[dim])
        up = [(i, (i + 1) % size) for i in range(size - 1)]
        down = [(j, i) for i, j in up]
        last = lax.slice_in_dim(array, length - width, length, axis=dim)
        initial = lax.slice_in_dim(array, 0, width, axis=dim)
        before = lax.ppermute(last, axis, up)
        after = lax.ppermute(initial, axis, down)
        array = jnp.concatenate([before, array, after], axis=dim)
    return array


def frame_rates(decay_codes, frame_count):
    levels = jnp.arange(LEVELS, dtype=jnp.int32)
    log_table = LOW_LOG + levels.astype(jnp.float32) / (LEVELS - 1) * (HIGH_LOG - LOW_LOG)
    picked = (decay_codes[:, None] == levels[None, :]).astype(jnp.float32)
    log_rate = jnp.sum(picked * log_table[None, :], axis=1)
    return jnp.exp(WINDOW / frame_count * log_rate)


def conv_rows(rows, weight):
    count, height, width = (rows.shape[0], rows.shape[1] - 2, rows.shape[2])
    padded = jnp.pad(rows, ((0, 0), (0, 0), (1, 1), (0, 0)))
    total = jnp.zeros((count, height, width, weight.shape[3]), jnp.float32)
    for i in range(3):
        for j in range(3):
            total = total + jnp.einsum(
                "frwc,ck->frwk",
                padded[:, i : i + height, j : j + width],
                weight[i, j],
                preferred_element_type=jnp.float32,
            )
    return total


def carry_combine(earlier, later):
    return (earlier[0] * later[0], later[0][None, None, :] * earlier[1] + later[1])


def recurrence(drive, gates):

    def advance(carry, inputs):
        state, product = carry
        frame_drive, gate = inputs
        state = gate[None, None, :] * state + frame_drive
        product = product * gate
        return ((state, product), (state, product))

    start = (jnp.zeros(drive.shape[1:], jnp.float32), jnp.ones((drive.shape[3],), jnp.float32))
    (last_state, last_product), (states, products) = lax.scan(advance, start, (drive, gates))
    identity = (jnp.ones_like(last_product), jnp.zeros_like(last_state))
    before_product, before_state = entering(
        (last_product, last_state), "tm", carry_combine, identity
    )
    return states + products[:, None, None, :] * before_state[None]


def on_device(frames, w_in, w_out, decay_codes, resets):
    frame_count = frames.shape[0] * lax.axis_size("tm")
    rates = frame_rates(decay_codes, frame_count)
    gates = (1.0 - resets.astype(jnp.float32))[:, None] * rates[None, :]
    extended = extended_2(frames, (("row", 1),), 1)
    state = recurrence(
        conv_rows(extended, lax.all_gather(w_in, ("tm", "row"), axis=3, tiled=True)), gates
    )
    hidden = jax.nn.gelu(state).astype(jnp.bfloat16)
    hidden_rows = extended_2(hidden, (("row", 1),), 1)
    return conv_rows(hidden_rows, lax.all_gather(w_out, ("tm", "row"), axis=3, tiled=True)).astype(
        jnp.bfloat16
    )


def solution(mesh):
    return jax.shard_map(
        on_device,
        mesh=mesh,
        in_specs=(
            P(("grp", "tm"), "row", None, None),
            P(None, None, None, ("tm", "row")),
            P(None, None, None, ("tm", "row")),
            P(),
            P(("grp", "tm")),
        ),
        out_specs=P(("grp", "tm"), "row", None, None),
        check_vma=False,
    )
```

profile of v0, /device:TPU:0, one launch (start us, length us, event | category | flops | bytes accessed | tf_op | source)
XLA Modules:
  0.0 140.0 jit_solution(1108490326736602466)
XLA Ops:
  6.5 0.0 copy-start
  6.5 0.0 all-gather.6.cloned.1.call-start
  6.5 0.7 all-gather.6.cloned.1.call-update
  7.3 0.0 all-gather.8.cloned.1.call-start
  7.3 0.7 all-gather.8.cloned.1.call-update
  8.0 0.8 fusion.50
  8.8 2.4 %collective-permute-start = (bf16[2,1,24,512]{3,2,1,0:T(8,128)(2,1)S(1)}, bf16[2,1,24,512]{3,2,1,0:T(8,128)(2,1)S(1)}, u32[]{:S(2)}, u32[]{:S(2)}) collective-permute-start(bf16[2,1,24,512]{3,2,1,0:T(8,128)(2,1)S(1)} %get-tuple-element.146), channel_id=1, source_target_pairs={{0,1},{1,2},{2,3},{4,5},{5,6},{6,7},{8,9},{9,10},{10,11},{12,13},{... | collective-permute-start | bytes 147464 | tf_op jit(solution)/shard_map/ppermute | solution.py:33
  11.2 1.3 collective-permute-start.1
  12.6 0.8 select_reduce_fusion
  13.3 0.7 convert_subtract_fusion
  14.0 0.1 broadcast_multiply_fusion
  14.1 0.0 collective-permute-done
  14.1 2.4 %collective-permute-done.1 = bf16[2,1,24,512]{3,2,1,0:T(8,128)(2,1)S(1)} collective-permute-done((bf16[2,1,24,512]{3,2,1,0:T(8,128)(2,1)S(1)}, bf16[2,1,24,512]{3,2,1,0:T(8,128)(2,1)S(1)}, u32[]{:S(2)}, u32[]{:S(2)}) %collective-permute-start.1) | collective-permute-done | bytes 49184 | tf_op jit(solution)/shard_map/ppermute | solution.py:34
  16.5 1.0 fusion.12
  17.4 47.8 %all-gather.6.cloned.1.call-done = bf16[3,3,512,512]{2,3,1,0:T(8,128)(2,1)} async-done(((bf16[3,3,512,32]{2,3,1,0:T(8,128)(2,1)}), bf16[3,3,512,512]{2,3,1,0:T(8,128)(2,1)}) %all-gather.6.cloned.1.call-update) | async-done | bytes 4718608 | tf_op jit(solution)/shard_map/all_gather | solution.py:90
  65.2 1.4 fusion.6
  66.6 1.3 fusion.5
  67.9 1.3 convolution_add_fusion.13
  69.3 1.3 convolution_add_fusion.12
  70.6 1.3 convolution_add_fusion.11
  72.0 0.0 copy-done
  72.0 1.4 convolution_add_fusion.10
  73.3 1.4 convolution_add_fusion.9
  74.7 1.3 convolution_add_fusion.8
  76.0 1.3 fusion.1
  77.4 0.3 while.30
  77.7 12.0 %all-gather.2 = f32[4,1,512]{2,1,0:T(1,128)S(1)} all-gather(f32[1,1,512]{2,1,0:T(1,128)S(1)} %bitcast.175), channel_id=2, replica_groups=mesh['grp'=2,'tm'=4,'row'=4] {'tm'}, dimensions={0}, use_global_device_ids=true | all-gather | bytes 10240 | tf_op jit(solution)/shard_map/all_gather | solution.py:15
  89.6 17.5 %all-gather.1 = f32[8,24,512]{2,1,0:T(8,128)S(1)} all-gather(f32[2,24,512]{2,1,0:T(8,128)S(1)} %get-tuple-element.92), channel_id=3, replica_groups=mesh['grp'=2,'tm'=4,'row'=4] {'tm'}, dimensions={0}, use_global_device_ids=true | all-gather | bytes 491520 | tf_op jit(solution)/shard_map/all_gather | solution.py:15
  107.2 0.1 fusion.20
  107.3 1.3 collective-permute-start.2
  108.6 1.3 collective-permute-start.3
  109.9 10.5 %all-gather.8.cloned.1.call-done = bf16[3,3,512,512]{2,3,1,0:T(8,128)(2,1)} async-done(((bf16[3,3,512,32]{2,3,1,0:T(8,128)(2,1)}), bf16[3,3,512,512]{2,3,1,0:T(8,128)(2,1)}) %all-gather.8.cloned.1.call-update) | async-done | bytes 4718608 | tf_op jit(solution)/shard_map/all_gather | solution.py:94
  120.3 0.0 collective-permute-done.2
  120.3 1.3 fusion.4
  121.7 0.0 collective-permute-done.3
  121.7 0.1 select_maximum_fusion
  121.8 1.3 fusion.3
  123.1 1.3 convolution_add_fusion.7
  124.5 1.3 convolution_add_fusion.6
  125.8 1.3 convolution_add_fusion.5
  127.1 1.3 convolution_add_fusion.4
  128.5 1.3 convolution_add_fusion.3
  129.8 1.3 convolution_add_fusion.2
  131.2 2.0 %fusion.2 = bf16[2,2,24,512]{3,2,1,0:T(8,128)(2,1)} fusion(f32[2,2,24,512]{3,2,1,0:T(8,128)S(1)} %fusion.3, f32[2,2,24,512]{3,2,1,0:T(8,128)S(1)} %convolution_add_fusion.2, bf16[3,3,512,512]{2,3,1,0:T(8,128)(2,1)} %all-gather.8.cloned.1.call-done, bf16[2,1,24,512]{3,2,1,0:T(8,128)(2,1)S(1)} %collective-permute-done.3, bf16[2,2,24,512]{3,2,1,0:T(8,128)(2,1)S(1)} %fusion.20), kind=kOutput, calls=%fused_computation.23 | convolution fusion | flops 50774016 | bytes 1163264 | tf_op jit(solution)/shard_map/frwc,ck->frwk/dot_general | solution.py:53
  (18 shorter events, 0.2 us)
Async XLA Ops:
  6.5 65.4 %copy-start = (bf16[2,2,24,512]{3,2,1,0:T(8,128)(2,1)S(1)}, bf16[2,2,24,512]{3,2,1,0:T(8,128)(2,1)}, u32[]{:S(2)}) copy-start(bf16[2,2,24,512]{3,2,1,0:T(8,128)(2,1)} %param.9) | copy-start | bytes 294916
  6.5 58.7 %all-gather.6.cloned.1.call-start = ((), (), s32[]{:S(2)}) async-start(), calls=%async_computation | async-start | bytes 5013504 | tf_op jit(solution)/shard_map/all_gather | solution.py:90
  7.3 113.1 %all-gather.8.cloned.1.call-start = ((), (), s32[]{:S(2)}) async-start(), calls=%async_computation.1 | async-start | bytes 5013504 | tf_op jit(solution)/shard_map/all_gather | solution.py:94
  8.8 5.2 %collective-permute-start = (bf16[2,1,24,512]{3,2,1,0:T(8,128)(2,1)S(1)}, bf16[2,1,24,512]{3,2,1,0:T(8,128)(2,1)S(1)}, u32[]{:S(2)}, u32[]{:S(2)}) collective-permute-start(bf16[2,1,24,512]{3,2,1,0:T(8,128)(2,1)S(1)} %get-tuple-element.146), channel_id=1, source_target_pairs={{0,1},{1,2},{2,3},{4,5},{5,6},{6,7},{8,9},{9,10},{10,11},{12,13},{... | collective-permute-start | bytes 147464 | tf_op jit(solution)/shard_map/ppermute | solution.py:33
  11.2 5.2 %collective-permute-start.1 = (bf16[2,1,24,512]{3,2,1,0:T(8,128)(2,1)S(1)}, bf16[2,1,24,512]{3,2,1,0:T(8,128)(2,1)S(1)}, u32[]{:S(2)}, u32[]{:S(2)}) collective-permute-start(bf16[2,1,24,512]{3,2,1,0:T(8,128)(2,1)S(1)} %get-tuple-element.147), channel_id=1, source_target_pairs={{1,0},{2,1},{3,2},{5,4},{6,5},{7,6},{9,8},{10,9},{11,10},{13,12},{... | collective-permute-start | bytes 147464 | tf_op jit(solution)/shard_map/ppermute | solution.py:34
  107.3 13.1 %collective-permute-start.2 = (bf16[2,1,24,512]{3,2,1,0:T(8,128)(2,1)S(1)}, bf16[2,1,24,512]{3,2,1,0:T(8,128)(2,1)S(1)}, u32[]{:S(2)}, u32[]{:S(2)}) collective-permute-start(bf16[2,1,24,512]{3,2,1,0:T(8,128)(2,1)S(1)} %get-tuple-element.144), channel_id=1, source_target_pairs={{0,1},{1,2},{2,3},{4,5},{5,6},{6,7},{8,9},{9,10},{10,11},{12,13},{... | collective-permute-start | bytes 147464 | tf_op jit(solution)/shard_map/ppermute | solution.py:33
  108.6 13.1 %collective-permute-start.3 = (bf16[2,1,24,512]{3,2,1,0:T(8,128)(2,1)S(1)}, bf16[2,1,24,512]{3,2,1,0:T(8,128)(2,1)S(1)}, u32[]{:S(2)}, u32[]{:S(2)}) collective-permute-start(bf16[2,1,24,512]{3,2,1,0:T(8,128)(2,1)S(1)} %get-tuple-element.145), channel_id=1, source_target_pairs={{1,0},{2,1},{3,2},{5,4},{6,5},{7,6},{9,8},{10,9},{11,10},{13,12},{... | collective-permute-start | bytes 147464 | tf_op jit(solution)/shard_map/ppermute | solution.py:34
Sparse Core Ops, SparseCore 0:
  9.5 55.6 all-gather.5
  67.4 52.8 all-gather.7
where the time goes:
time: 141 us; the launch traced here: 140 us
  waiting for transfers between devices  62.1 us (44%)
  blocking collectives  29.5 us (21%)
  matrix products  24.8 us (18%)
  between operations  13.6 us (10%)
  starting transfers between devices  6.3 us (4%)
  other arithmetic  2.76 us (2%)
    all_gather x1, waiting for transfers between devices, on_device(): lax.all_gather(w_in, ('tm', 'row'), axis=3, tiled=True)  47.8 us
    all_gather x2, blocking collectives, entering(): gathered = jax.tree.map(lambda a: lax.all_gather(a, axis), part)  29.5 us
    dot_general x18, matrix products, conv_rows(): jnp.einsum('frwc,ck->frwk', padded[:, i:i + height, j:j + width], weight[...  24.8 us
    all_gather x1, waiting for transfers between devices, on_device(): lax.all_gather(w_out, ('tm', 'row'), axis=3, tiled=True)  10.5 us
    ppermute x2, starting transfers between devices, extended_2(): before = lax.ppermute(last, axis, up)  3.68 us
  transfers between devices with their start and end apart: 6, of which 3 were waited for; matrix products, arithmetic and copies ran while one was open for 12% of the time, Pallas kernels for 0%

commit v1 on v0

--- a/solution.py
+++ b/solution.py
@@ -87,7 +87,16 @@
     gates = (1.0 - resets.astype(jnp.float32))[:, None] * rates[None, :]
     extended = extended_2(frames, (("row", 1),), 1)
     state = recurrence(
-        conv_rows(extended, lax.all_gather(w_in, ("tm", "row"), axis=3, tiled=True)), gates
+        conv_rows(
+            extended,
+            jnp.concatenate(
+                lax.all_to_all(
+                    jnp.stack([w_in] * lax.axis_size(("tm", "row"))), ("tm", "row"), 0, 0
+                ),
+                axis=3,
+            ),
+        ),
+        gates,
     )
     hidden = jax.nn.gelu(state).astype(jnp.bfloat16)
     hidden_rows = extended_2(hidden, (("row", 1),), 1)

time: 141 us -> 209 us (1.48)
  waiting for transfers between devices: 62.1 us -> 112 us
  blocking collectives: 29.5 us -> 43.9 us
  matrix products: 24.8 us -> 15.3 us
  starting transfers between devices: 6.3 us -> 13.7 us
  local copies, waits for them, and re-layouts: 0.97 us -> 6.65 us
  other arithmetic: 2.76 us -> 0.53 us
    all_to_all x0 -> x1, waiting for transfers between devices: none -> 108 us  [on_device(): lax.all_to_all(jnp.stack([w_in] * lax.axis_size(('tm', 'row'))), ('tm', '...]
    all_gather x1 -> x0, waiting for transfers between devices: 47.8 us -> none  [on_device(): lax.all_gather(w_in, ('tm', 'row'), axis=3, tiled=True)]
    all_gather x2, blocking collectives: 29.5 us -> 43.9 us  [entering(): gathered = jax.tree.map(lambda a: lax.all_gather(a, axis), part)]
    all_gather x1, waiting for transfers between devices: 10.5 us -> 0.02 us  [on_device(): lax.all_gather(w_out, ('tm', 'row'), axis=3, tiled=True)]
    dot_general x18, matrix products: 24.8 us -> 15.3 us  [conv_rows(): jnp.einsum('frwc,ck->frwk', padded[:, i:i + height, j:j + width], weight[...]
    all_to_all x0 -> x1, starting transfers between devices: none -> 7.56 us  [on_device(): lax.all_to_all(jnp.stack([w_in] * lax.axis_size(('tm', 'row'))), ('tm', '...]
    another operation x1 -> x2, local copies, waits for them, and re-layouts: 0.01 us -> 3.78 us  [the longest x1 3.77 us: on_device(): jnp.stack([w_in] * lax.axis_size(('tm', 'row')))]
    all_to_all x0 -> x1, local copies, waits for them, and re-layouts: none -> 2.74 us  [on_device(): lax.all_to_all(jnp.stack([w_in] * lax.axis_size(('tm', 'row'))), ('tm', '...]
  transfers between devices with their start and end apart: 6 -> 6, of which waited for: 3 -> 3; matrix products, arithmetic and copies ran while one was open for 12% -> 4% of each run, Pallas kernels for 0% -> 0%
where the time goes in v1:
time: 209 us; the launch traced here: 206 us
  waiting for transfers between devices  112 us (54%)
  blocking collectives  43.9 us (21%)
  matrix products  15.3 us (7%)
  starting transfers between devices  13.7 us (7%)
  between operations  13.6 us (7%)
  local copies, waits for them, and re-layouts  6.65 us (3%)
    all_to_all x1, waiting for transfers between devices, on_device(): lax.all_to_all(jnp.stack([w_in] * lax.axis_size(('tm', 'row'))), ('tm', '...  108 us
    all_gather x2, blocking collectives, entering(): gathered = jax.tree.map(lambda a: lax.all_gather(a, axis), part)  43.9 us
    dot_general x18, matrix products, conv_rows(): jnp.einsum('frwc,ck->frwk', padded[:, i:i + height, j:j + width], weight[...  15.3 us
    all_to_all x1, starting transfers between devices, on_device(): lax.all_to_all(jnp.stack([w_in] * lax.axis_size(('tm', 'row'))), ('tm', '...  7.56 us
  transfers between devices with their start and end apart: 6, of which 3 were waited for; matrix products, arithmetic and copies ran while one was open for 4% of the time, Pallas kernels for 0%

profile of v1, /device:TPU:0, one launch (start us, length us, event | category | flops | bytes accessed | tf_op | source)
XLA Modules:
  0.0 206.3 jit_solution(10130722589534699400)
XLA Ops:
  6.5 3.8 %stack.2 = bf16[16,3,3,512,32]{3,4,2,1,0:T(8,128)(2,1)} broadcast(bf16[3,3,512,32]{2,3,1,0:T(8,128)(2,1)} %param.10), dimensions={1,2,3,4} | broadcast | bytes 5013504 | tf_op jit(solution)/shard_map/stack | solution.py:94
  10.3 0.0 copy-start
  10.3 0.0 copy-start.1
  10.3 0.0 copy-start.2
  10.3 7.6 %all-to-all-start = ((bf16[16,3,3,512,32]{3,4,2,1,0:T(8,128)(2,1)}), bf16[16,3,3,512,32]{3,4,2,1,0:T(8,128)(2,1)}, u32[]{:S(2)}, u32[]{:S(2)}) async-start(bf16[16,3,3,512,32]{3,4,2,1,0:T(8,128)(2,1)} %stack.2), calls=%async_computation | async-start | bytes 9437184 | tf_op jit(solution)/shard_map/all_to_all | solution.py:93
  17.9 0.0 all-gather.5.cloned.1.call-start
  17.9 0.7 all-gather.5.cloned.1.call-update
  18.6 0.0 copy-done
  18.6 2.3 %collective-permute-start = (bf16[2,1,24,512]{3,2,1,0:T(8,128)(2,1)S(1)}, bf16[2,1,24,512]{3,2,1,0:T(8,128)(2,1)S(1)}, u32[]{:S(2)}, u32[]{:S(2)}) collective-permute-start(bf16[2,1,24,512]{3,2,1,0:T(8,128)(2,1)S(1)} %get-tuple-element.146), channel_id=1, source_target_pairs={{0,1},{1,2},{2,3},{4,5},{5,6},{6,7},{8,9},{9,10},{10,11},{12,13},{... | collective-permute-start | bytes 147464 | tf_op jit(solution)/shard_map/ppermute | solution.py:33
  20.9 1.3 collective-permute-start.1
  22.2 0.0 copy-done.1
  22.2 0.1 select_reduce_fusion
  22.3 0.0 copy-done.2
  22.3 0.1 broadcast_multiply_fusion
  22.4 0.0 collective-permute-done
  22.4 2.7 %collective-permute-done.1 = bf16[2,1,24,512]{3,2,1,0:T(8,128)(2,1)S(1)} collective-permute-done((bf16[2,1,24,512]{3,2,1,0:T(8,128)(2,1)S(1)}, bf16[2,1,24,512]{3,2,1,0:T(8,128)(2,1)S(1)}, u32[]{:S(2)}, u32[]{:S(2)}) %collective-permute-start.1) | collective-permute-done | bytes 49184 | tf_op jit(solution)/shard_map/ppermute | solution.py:34
  25.2 0.1 fusion.12
  25.3 107.7 %all-to-all-done = bf16[16,3,3,512,32]{3,4,2,1,0:T(8,128)(2,1)} async-done(((bf16[16,3,3,512,32]{3,4,2,1,0:T(8,128)(2,1)}), bf16[16,3,3,512,32]{3,4,2,1,0:T(8,128)(2,1)}, u32[]{:S(2)}, u32[]{:S(2)}) %all-to-all-start) | async-done | bytes 4718624 | tf_op jit(solution)/shard_map/all_to_all | solution.py:93
  133.0 2.7 %copy.37 = bf16[16,3,3,512,32]{3,4,0,2,1:T(8,128)(2,1)S(1)} copy(bf16[16,3,3,512,32]{3,4,2,1,0:T(8,128)(2,1)} %all-to-all-done) | data formatting | bytes 9437184 | tf_op jit(solution)/shard_map/all_to_all | solution.py:93
  135.7 0.3 fusion.6
  136.0 0.3 fusion.5
  136.3 0.3 convolution_add_fusion.13
  136.6 0.3 convolution_add_fusion.12
  136.9 0.3 convolution_add_fusion.11
  137.2 0.3 convolution_add_fusion.10
  137.5 0.3 convolution_add_fusion.9
  137.8 0.3 convolution_add_fusion.8
  138.1 0.3 fusion.1
  138.4 0.3 while.30
  138.7 29.6 %all-gather.2 = f32[4,1,512]{2,1,0:T(1,128)S(1)} all-gather(f32[1,1,512]{2,1,0:T(1,128)S(1)} %bitcast.187), channel_id=2, replica_groups=mesh['grp'=2,'tm'=4,'row'=4] {'tm'}, dimensions={0}, use_global_device_ids=true | all-gather | bytes 10240 | tf_op jit(solution)/shard_map/all_gather | solution.py:15
  168.3 14.3 %all-gather.1 = f32[8,24,512]{2,1,0:T(8,128)S(1)} all-gather(f32[2,24,512]{2,1,0:T(8,128)S(1)} %get-tuple-element.92), channel_id=3, replica_groups=mesh['grp'=2,'tm'=4,'row'=4] {'tm'}, dimensions={0}, use_global_device_ids=true | all-gather | bytes 491520 | tf_op jit(solution)/shard_map/all_gather | solution.py:15
  182.6 0.1 fusion.20
  182.7 1.3 collective-permute-start.2
  184.0 1.3 collective-permute-start.3
  185.3 0.0 all-gather.5.cloned.1.call-done
  185.3 0.0 collective-permute-done.2
  185.4 1.3 fusion.4
  186.7 1.3 collective-permute-done.3
  188.0 0.1 select_maximum_fusion
  188.1 1.3 fusion.3
  189.4 1.3 convolution_add_fusion.7
  190.8 1.3 convolution_add_fusion.6
  192.1 1.3 convolution_add_fusion.5
  193.5 1.3 convolution_add_fusion.4
  194.8 1.3 convolution_add_fusion.3
  196.2 1.3 convolution_add_fusion.2
  197.5 2.0 fusion.2
  (20 shorter events, 0.3 us)
Async XLA Ops:
  10.3 8.3 %copy-start = (bf16[2,2,24,512]{3,2,1,0:T(8,128)(2,1)S(1)}, bf16[2,2,24,512]{3,2,1,0:T(8,128)(2,1)}, u32[]{:S(2)}) copy-start(bf16[2,2,24,512]{3,2,1,0:T(8,128)(2,1)} %param.9) | copy-start | bytes 294916
  10.3 11.9 %copy-start.1 = (s32[512]{0:T(512)S(1)}, s32[512]{0:T(512)}, u32[]{:S(2)}) copy-start(s32[512]{0:T(512)} %param.12) | copy-start | bytes 6148
  10.3 12.0 %copy-start.2 = (s32[2]{0:T(128)S(1)}, s32[2]{0:T(128)}, u32[]{:S(2)}) copy-start(s32[2]{0:T(128)} %param.13) | copy-start | bytes 28
  10.3 122.6 %all-to-all-start = ((bf16[16,3,3,512,32]{3,4,2,1,0:T(8,128)(2,1)}), bf16[16,3,3,512,32]{3,4,2,1,0:T(8,128)(2,1)}, u32[]{:S(2)}, u32[]{:S(2)}) async-start(bf16[16,3,3,512,32]{3,4,2,1,0:T(8,128)(2,1)} %stack.2), calls=%async_computation | async-start | bytes 9437184 | tf_op jit(solution)/shard_map/all_to_all | solution.py:93
  17.9 167.5 %all-gather.5.cloned.1.call-start = ((), (), s32[]{:S(2)}) async-start(), calls=%async_computation.1 | async-start | bytes 5013504 | tf_op jit(solution)/shard_map/all_gather | solution.py:103
  18.6 3.8 %collective-permute-start = (bf16[2,1,24,512]{3,2,1,0:T(8,128)(2,1)S(1)}, bf16[2,1,24,512]{3,2,1,0:T(8,128)(2,1)S(1)}, u32[]{:S(2)}, u32[]{:S(2)}) collective-permute-start(bf16[2,1,24,512]{3,2,1,0:T(8,128)(2,1)S(1)} %get-tuple-element.146), channel_id=1, source_target_pairs={{0,1},{1,2},{2,3},{4,5},{5,6},{6,7},{8,9},{9,10},{10,11},{12,13},{... | collective-permute-start | bytes 147464 | tf_op jit(solution)/shard_map/ppermute | solution.py:33
  20.9 4.3 %collective-permute-start.1 = (bf16[2,1,24,512]{3,2,1,0:T(8,128)(2,1)S(1)}, bf16[2,1,24,512]{3,2,1,0:T(8,128)(2,1)S(1)}, u32[]{:S(2)}, u32[]{:S(2)}) collective-permute-start(bf16[2,1,24,512]{3,2,1,0:T(8,128)(2,1)S(1)} %get-tuple-element.147), channel_id=1, source_target_pairs={{1,0},{2,1},{3,2},{5,4},{6,5},{7,6},{9,8},{10,9},{11,10},{13,12},{... | collective-permute-start | bytes 147464 | tf_op jit(solution)/shard_map/ppermute | solution.py:34
  182.7 2.6 %collective-permute-start.2 = (bf16[2,1,24,512]{3,2,1,0:T(8,128)(2,1)S(1)}, bf16[2,1,24,512]{3,2,1,0:T(8,128)(2,1)S(1)}, u32[]{:S(2)}, u32[]{:S(2)}) collective-permute-start(bf16[2,1,24,512]{3,2,1,0:T(8,128)(2,1)S(1)} %get-tuple-element.144), channel_id=1, source_target_pairs={{0,1},{1,2},{2,3},{4,5},{5,6},{6,7},{8,9},{9,10},{10,11},{12,13},{... | collective-permute-start | bytes 147464 | tf_op jit(solution)/shard_map/ppermute | solution.py:33
  184.0 4.0 %collective-permute-start.3 = (bf16[2,1,24,512]{3,2,1,0:T(8,128)(2,1)S(1)}, bf16[2,1,24,512]{3,2,1,0:T(8,128)(2,1)S(1)}, u32[]{:S(2)}, u32[]{:S(2)}) collective-permute-start(bf16[2,1,24,512]{3,2,1,0:T(8,128)(2,1)S(1)} %get-tuple-element.145), channel_id=1, source_target_pairs={{1,0},{2,1},{3,2},{5,4},{6,5},{7,6},{9,8},{10,9},{11,10},{13,12},{... | collective-permute-start | bytes 147464 | tf_op jit(solution)/shard_map/ppermute | solution.py:34
Sparse Core Ops, SparseCore 0:
  20.9 103.4 all-gather.4
